TPU v7x, 32 devices: a whole 2x2x4 slice. The times are simulated.
32 devices in a mesh: dish: 4 (over y, x), chan: 8 (over z, core).
Axes of the slice: x: 2, y: 2, z: 4, core: 2. Of those that a mesh axis runs over, the one named last changes fastest.
Arguments:
- voltages: bfloat16 [2, 64, 4096, 512], P(None, 'dish', 'chan'), may hold values from -150 to 150
- beam_weights: bfloat16 [2, 4096, 64, 1024], P(None, ('chan', 'dish')), may hold values from -0.5 to 0.5
- flags: int32 [4096], P('chan'), may hold values 0 or 1
- sk_bins: int32 [4096], P('chan'), may hold values from 1 to 8
- bin_of_sample: int32 [512], replicated, may hold values from 0 to 63, never falling along the last dimension, each value on 1 to 16 neighbouring positions
Outputs:
- beam_power: bfloat16 [4096, 65536], P(None, ('dish', 'chan'))
Inputs may be any that keep to these rules, and one draw needn't show every extreme that they name: `bin_of_sample`: never falls; each of the 64 bins holds 1 to 16 samples.
All inputs are finite; a program needn't handle non-finite values. No bound on the sum of `flags` on one device may be relied on, other than what follows from the above.
Results may differ from a plain program's by a relative error of at most 0.006.
Values may be sent and summed in bfloat16 or wider, within the bound.
A program may use at most 192 MiB of HBM per device.

v0:
```python
import jax
import jax.numpy as jnp
from jax import lax
from jax.sharding import PartitionSpec as P

TBINS = 64


def kurtosis_scale(first_sum, second_sum, samples, flags, sk_bins):
    widths = 0.05 * sk_bins.astype(jnp.float32)
    mean_one = first_sum / samples
    mean_two = second_sum / samples
    ratio = mean_two / (mean_one * mean_one + 1e-06)
    kurtosis = (samples + 1.0) / (samples - 1.0) * (ratio - 1.0)
    excess = kurtosis - 1.0
    return flags.astype(jnp.float32) * widths / (widths + excess * excess)


def moment_sums(volts):
    floats = volts.astype(jnp.float32)
    powers = floats[0] * floats[0] + floats[1] * floats[1]
    return (jnp.sum(powers, axis=(0, 2)), jnp.sum(powers * powers, axis=(0, 2)))


def apply_scale(volts, scaling):
    return (volts.astype(jnp.float32) * scaling[None, None, :, None]).astype(jnp.bfloat16)


def channel_average(volts, weights, onehot, counts):
    stacked_v = jnp.concatenate([volts[0], volts[1]], axis=0)
    real_rows = jnp.concatenate([weights[0], -weights[1]], axis=0)
    imag_rows = jnp.concatenate([weights[1], weights[0]], axis=0)
    stacked_w = jnp.concatenate([real_rows, imag_rows], axis=1)
    beam_volts = jnp.dot(stacked_w.T, stacked_v, preferred_element_type=jnp.float32)
    half = weights.shape[2]
    real_part = beam_volts[:half]
    imag_part = beam_volts[half:]
    powers = real_part * real_part + imag_part * imag_part
    upper = powers.astype(jnp.bfloat16)
    lower = (powers - upper.astype(jnp.float32)).astype(jnp.bfloat16)
    summed = jnp.dot(upper, onehot, preferred_element_type=jnp.float32) + jnp.dot(
        lower, onehot, preferred_element_type=jnp.float32
    )
    return (summed / counts[None, :]).astype(jnp.bfloat16)


def body(voltages, beam_weights, flags, sk_bins, bin_of_sample):
    dish_count = lax.axis_size("dish")
    chan_count = lax.axis_size("chan")
    samples = float(voltages.shape[1] * dish_count * voltages.shape[3])
    first_sum, second_sum = moment_sums(voltages)
    first_sum, second_sum = lax.psum((first_sum, second_sum), "dish")
    scaling = kurtosis_scale(first_sum, second_sum, samples, flags, sk_bins)
    turned = lax.all_to_all(
        apply_scale(voltages, scaling), "dish", split_axis=2, concat_axis=1, tiled=True
    )
    chan_here = turned.shape[2]
    matches = bin_of_sample[:, None] == jnp.arange(TBINS, dtype=jnp.int32)[None, :]
    onehot = matches.astype(jnp.bfloat16)
    counts = jnp.sum(matches.astype(jnp.float32), axis=0)

    def one_channel(index):
        volts = lax.dynamic_index_in_dim(turned, index, 2, keepdims=False)
        weights = lax.dynamic_index_in_dim(beam_weights, index, 1, keepdims=False)
        return channel_average(volts, weights, onehot, counts)

    averaged = lax.map(one_channel, jnp.arange(chan_here, dtype=jnp.int32))
    beam_total = beam_weights.shape[3]
    per_owner = beam_total // (dish_count * chan_count)
    blocks = averaged.reshape(1, 1, chan_here, dish_count, chan_count, per_owner * TBINS)
    moved = lax.all_to_all(
        lax.all_to_all(blocks, "dish", split_axis=3, concat_axis=1, tiled=True),
        "chan",
        split_axis=4,
        concat_axis=0,
        tiled=True,
    )
    return moved.reshape(chan_count * dish_count * chan_here, per_owner * TBINS)


def solution(mesh):
    in_specs = (
        P(None, "dish", "chan", None),
        P(None, ("chan", "dish"), None, None),
        P("chan"),
        P("chan"),
        P(),
    )
    out_specs = P(None, ("dish", "chan"))
    return jax.shard_map(body, mesh=mesh, in_specs=in_specs, out_specs=out_specs, check_vma=False)
```

profile of v0, /device:TPU:0, one launch (start us, length us, event | category | flops | bytes accessed | tf_op | source)
XLA Modules:
  0.0 1813.8 jit_solution(3477855114896970488)
XLA Ops:
  0.0 14.7 copy_convert_fusion
  14.8 5.7 multiply_reduce_fusion
  20.5 11.4 all-reduce
  31.9 19.8 %multiply_convert_fusion = bf16[2,16,512,512]{3,1,0,2:T(8,128)(2,1)} fusion(f32[512]{0:T(512)S(1)} %add_divide_fusion, bf16[2,16,512,512]{3,2,1,0:T(8,128)(2,1)} %param.7), kind=kLoop, calls=%fused_computation.33 | loop fusion | flops 25165824 | bytes 33556480 | tf_op jit(solution)/shard_map/convert_element_type | solution.py:26
  51.7 7.1 all-to-all-start
  58.9 180.4 %all-to-all-done = bf16[2,16,512,512]{3,1,0,2:T(8,128)(2,1)} async-done(((bf16[2,16,512,512]{3,1,0,2:T(8,128)(2,1)}), bf16[2,16,512,512]{3,1,0,2:T(8,128)(2,1)}, u32[]{:S(2)}, u32[]{:S(2)}) %all-to-all-start) | async-done | bytes 16777248 | tf_op jit(solution)/shard_map/all_to_all | solution.py:54
  239.3 14.2 copy.20
  253.5 955.0 %while.11 = (s32[]{:T(128)}, bf16[128,1024,64]{1,2,0:T(8,128)(2,1)}, s32[128]{0:T(128)S(1)}, bf16[2,128,64,1024]{3,2,1,0:T(8,128)(2,1)}, bf16[2,64,128,512]{3,1,...) while((s32[]{:T(128)}, ...), condition=%wide.region_6.7_spmd.clone, body=%wide.region_5.6_spmd.clone.sunk | while | flops 411172864 | bytes 14685115 | solution.py:67
  259.8 1.2 fusion.49
  267.2 1.2 fusion.49
  274.7 1.2 fusion.49
  282.1 1.2 fusion.49
  289.6 1.2 fusion.49
  297.1 1.2 fusion.49
  312.0 1.2 fusion.49
  319.4 1.2 fusion.49
  334.4 1.2 fusion.49
  341.8 1.2 fusion.49
  356.7 1.2 fusion.49
  364.2 1.2 fusion.49
  371.7 1.2 fusion.49
  379.1 1.2 fusion.49
  394.0 1.2 fusion.49
  401.5 1.2 fusion.49
  416.4 1.2 fusion.49
  423.9 1.2 fusion.49
  431.4 1.2 fusion.49
  1208.5 26.0 %copy.21 = bf16[128,1024,64]{0,2,1:T(8,128)(2,1)} copy(bf16[128,1024,64]{1,2,0:T(8,128)(2,1)} %get-tuple-element.42) | data formatting | bytes 33554432 | tf_op jit(solution)/shard_map/while | solution.py:67
  1234.5 186.9 %all_to_all.51 = bf16[1,1,128,4,8,2048]{2,5,4,1,0,3:T(8,128)(2,1)S(1)} all-to-all(bf16[1,1,128,4,8,2048]{2,5,4,1,0,3:T(8,128)(2,1)} %bitcast.39), channel_id=1, replica_groups=mesh['dish'=4,'chan'=8] {'dish'}, dimensions={3} | all-to-all | bytes 33554432 | tf_op jit(solution)/shard_map/all_to_all | solution.py:72
  1421.4 2.5 copy.23
  1423.9 368.4 %all_to_all.52 = bf16[1,4,128,1,8,2048]{2,5,1,3,0,4:T(8,128)(2,1)} all-to-all(bf16[1,4,128,1,8,2048]{2,5,1,3,0,4:T(8,128)(2,1)S(1)} %copy.23), channel_id=1, replica_groups=mesh['dish'=4,'chan'=8] {'chan'}, dimensions={4} | all-to-all | bytes 33554432 | tf_op jit(solution)/shard_map/all_to_all | solution.py:71
  1792.3 21.5 %copy.24 = bf16[1,4,128,1,8,2048]{5,2,1,4,3,0:T(8,128)(2,1)} copy(bf16[1,4,128,1,8,2048]{2,5,1,3,0,4:T(8,128)(2,1)} %all_to_all.52) | data formatting | bytes 33554432 | tf_op jit(solution)/shard_map/all_to_all | solution.py:71
  (887 shorter events, 714.3 us)
Async XLA Ops:
  14.8 17.1 copy-start
  14.8 17.1 copy-start.1
  51.7 7.1 copy-start.2
  51.7 187.6 %all-to-all-start = ((bf16[2,16,512,512]{3,1,0,2:T(8,128)(2,1)}), bf16[2,16,512,512]{3,1,0,2:T(8,128)(2,1)}, u32[]{:S(2)}, u32[]{:S(2)}) async-start(bf16[2,16,512,512]{3,1,0,2:T(8,128)(2,1)} %multiply_convert_fusion), calls=%async_computation | async-start | bytes 33554432 | tf_op jit(solution)/shard_map/all_to_all | solution.py:54
where the time goes:
time: 1830 us; the launch traced here: 1810 us
  blocking collectives  567 us (31%)
  local copies, waits for them, and re-layouts  370 us (20%)
  matrix products  313 us (17%)
  loops' own time  218 us (12%)
  waiting for transfers between devices  180 us (10%)
  other arithmetic  159 us (9%)
    all_to_all x1, blocking collectives, body(): lax.all_to_all(lax.all_to_all(blocks, 'dish', split_axis=3, concat_axis=1...  368 us
    another operation x1, loops' own time, body(): averaged = lax.map(one_channel, jnp.arange(chan_here, dtype=jnp.int32))  218 us
    all_to_all x1, blocking collectives, body(): lax.all_to_all(blocks, 'dish', split_axis=3, concat_axis=1, tiled=True)  187 us
    all_to_all x1, waiting for transfers between devices, body(): lax.all_to_all(apply_scale(voltages, scaling), 'dish', split_axis=2, conc...  180 us
    dot_general x128, matrix products, channel_average(): jnp.dot(lower, onehot, preferred_element_type=jnp.float32)  153 us
    neg x128, other arithmetic, channel_average(): real_rows = jnp.concatenate([weights[0], -weights[1]], axis=0)  119 us
    squeeze x128, local copies, waits for them, and re-layouts, channel_average(): real_rows = jnp.concatenate([weights[0], -weights[1]], axis=0)  118 us
    squeeze x128, local copies, waits for them, and re-layouts, channel_average(): stacked_v = jnp.concatenate([volts[0], volts[1]], axis=0)  114 us
  transfers between devices with their start and end apart: 1, of which 1 were waited for; matrix products, arithmetic and copies ran while one was open for 0% of the time, Pallas kernels for 0%

commit v1 on v0

v1 whole, which is shorter than its diff:
```python
import functools

import jax
import jax.numpy as jnp
from jax import lax
from jax.experimental import pallas as pl
from jax.experimental.pallas import tpu as pltpu
from jax.sharding import PartitionSpec as P

TBINS = 64
LANES = 128
MESH = pl.DeviceIdType.MESH


def kernel(
    nd, nc, group,
    vt_ref, w_ref, flag_ref, width_ref, onehot_ref, count_ref,
    out_ref,
    volts, wbuf, qbuf, rbuf, stage,
    own_sem, w_sem, send1, recv1, send3, recv3, self_sem,
):
    channels = vt_ref.shape[1]
    groups = channels // group
    dishes = w_ref.shape[2]
    beams = w_ref.shape[3]
    samples = vt_ref.shape[4]
    devices = nd * nc
    pairs = beams // 2
    own_pairs = pairs // devices
    me_d = lax.axis_index("dish")
    me_c = lax.axis_index("chan")
    me = me_d * nc + me_c
    my_row = (me_c * nd + me_d) * channels

    def volt_copy(g, off):
        peer = lax.rem(me_d + off, nd)
        return pltpu.make_async_remote_copy(
            src_ref=vt_ref.at[peer, pl.ds(g * group, group)],
            dst_ref=volts.at[me_d, pl.ds(g * group, group)],
            send_sem=send1.at[g, off],
            recv_sem=recv1.at[g, off],
            device_id=(peer, me_c),
            device_id_type=MESH,
        )

    def volt_arrival(g, off):
        source = lax.rem(me_d + nd - off, nd)
        here = volts.at[source, pl.ds(g * group, group)]
        return pltpu.make_async_remote_copy(
            src_ref=here, dst_ref=here, send_sem=send1.at[g, off], recv_sem=recv1.at[g, off],
            device_id=(source, me_c), device_id_type=MESH,
        )

    def own_copy(g):
        return pltpu.make_async_copy(
            vt_ref.at[me_d, pl.ds(g * group, group)], volts.at[me_d, pl.ds(g * group, group)], own_sem.at[g]
        )

    def weight_copy(g):
        slot = lax.rem(g, 2)
        return pltpu.make_async_copy(w_ref.at[:, pl.ds(g * group, group)], wbuf.at[slot], w_sem.at[slot])

    def start_volts(g, _):
        for off in range(1, nd):
            volt_copy(g, off).start()
        own_copy(g).start()
        return 0

    lax.fori_loop(0, groups, start_volts, 0)
    weight_copy(0).start()

    def result_copy(g, off):
        target = lax.rem(me + off, devices)
        return pltpu.make_async_remote_copy(
            src_ref=stage.at[g, target],
            dst_ref=out_ref.at[pl.ds(pl.multiple_of(my_row + g * group, group), group)],
            send_sem=send3.at[off],
            recv_sem=recv3.at[off],
            device_id=(target // nc, lax.rem(target, nc)),
            device_id_type=MESH,
        )

    def self_copy(g):
        return pltpu.make_async_copy(
            stage.at[g, me],
            out_ref.at[pl.ds(pl.multiple_of(my_row + g * group, group), group)],
            self_sem.at[g],
        )

    lane = lax.broadcasted_iota(jnp.int32, (pairs, LANES), 1)
    total = float(dishes * samples)
    block = min(256, beams)

    def one_group(g, _):
        slot = lax.rem(g, 2)

        @pl.when(g + 1 < groups)
        def _():
            weight_copy(g + 1).start()

        own_copy(g).wait()
        for off in range(1, nd):
            volt_arrival(g, off).wait_recv()
        weight_copy(g).wait()

        def one_channel(i, _):
            c = g * group + i
            both = volts[:, c]
            real = both[:, 0].reshape(dishes, samples)
            imag = both[:, 1].reshape(dishes, samples)
            real32 = real.astype(jnp.float32)
            imag32 = imag.astype(jnp.float32)
            power = real32 * real32 + imag32 * imag32
            one = jnp.sum(jnp.sum(power, axis=0, keepdims=True), axis=1, keepdims=True) / total
            two = jnp.sum(jnp.sum(power * power, axis=0, keepdims=True), axis=1, keepdims=True) / total
            ratio = two / (one * one + 1e-06)
            excess = (total + 1.0) / (total - 1.0) * (ratio - 1.0) - 1.0
            width = width_ref[c]
            scaling = flag_ref[c] * width / (width + excess * excess)
            factor = scaling * scaling / count_ref[...]
            right = jnp.concatenate(
                [jnp.concatenate([real, imag], axis=1), jnp.concatenate([-imag, real], axis=1)], axis=0
            )
            for at in range(0, beams, block):
                left = jnp.concatenate(
                    [wbuf[slot, 0, i, :, pl.ds(at, block)], wbuf[slot, 1, i, :, pl.ds(at, block)]], axis=0
                )
                beam = lax.dot_general(
                    left, right, (((0,), (0,)), ((), ())), preferred_element_type=jnp.float32
                )
                re = beam[:, :samples]
                im = beam[:, samples:]
                detected = (re * re + im * im).astype(jnp.bfloat16)
                binned = jnp.dot(detected, onehot_ref[...], preferred_element_type=jnp.float32)
                qbuf[pl.ds(at, block), :] = binned * factor
            even = qbuf[pl.ds(0, pairs, stride=2), :]
            odd = qbuf[pl.ds(1, pairs, stride=2), :]
            rbuf[pl.ds(i, pairs, stride=group), :] = jnp.where(lane < TBINS, even, odd)
            return 0

        lax.fori_loop(0, group, one_channel, 0)

        def one_target(j, _):
            for p in range(own_pairs):
                row = pl.multiple_of((j * own_pairs + p) * group, group)
                stage[g, j, :, pl.ds(p * LANES, LANES)] = rbuf[pl.ds(row, group), :].astype(jnp.bfloat16)
            return 0

        lax.fori_loop(0, devices, one_target, 0)

        def send(off, _):
            result_copy(g, off).start()
            return 0

        lax.fori_loop(1, devices, send, 0)
        self_copy(g).start()
        return 0

    lax.fori_loop(0, groups, one_group, 0)

    def finish(g, _):
        for off in range(1, nd):
            volt_copy(g, off).wait_send()
        self_copy(g).wait()
        return 0

    lax.fori_loop(0, groups, finish, 0)

    def drain(off, _):
        source = lax.rem(me + devices - off, devices)
        row = (lax.rem(source, nc) * nd + source // nc) * channels
        block_ref = out_ref.at[pl.ds(pl.multiple_of(row, group), channels)]
        landed = pltpu.make_async_remote_copy(
            src_ref=block_ref, dst_ref=block_ref, send_sem=send3.at[off], recv_sem=recv3.at[off],
            device_id=(source // nc, lax.rem(source, nc)), device_id_type=MESH,
        )
        landed.wait_send()
        landed.wait_recv()
        return 0

    lax.fori_loop(1, devices, drain, 0)


def solution(mesh):
    nd, nc = mesh.shape["dish"], mesh.shape["chan"]

    def body(voltages, beam_weights, flags, sk_bins, bin_of_sample):
        _, local_dishes, block_channels, samples = voltages.shape
        _, channels, dishes, beams = beam_weights.shape
        devices = nd * nc
        group = min(16, channels)
        groups = channels // group
        columns = beams // devices * TBINS
        vt = jnp.transpose(voltages, (2, 0, 1, 3)).reshape(nd, channels, 2, local_dishes, samples)
        start = lax.axis_index("dish") * channels
        spread = lambda x: jnp.broadcast_to(
            lax.dynamic_slice(x, (start,), (channels,)).astype(jnp.float32)[:, None, None], (channels, 1, LANES)
        )
        bins = jnp.arange(LANES, dtype=jnp.int32) % TBINS
        matches = bin_of_sample[:, None] == bins[None, :]
        onehot = matches.astype(jnp.bfloat16)
        counts = jnp.sum(matches.astype(jnp.float32), axis=0, keepdims=True)
        anywhere = pl.BlockSpec(memory_space=pl.ANY)
        local = pl.BlockSpec(memory_space=pltpu.VMEM)
        return pl.pallas_call(
            functools.partial(kernel, nd, nc, group),
            out_shape=jax.ShapeDtypeStruct((devices * channels, columns), jnp.bfloat16),
            in_specs=[anywhere, anywhere, local, local, local, local],
            out_specs=anywhere,
            scratch_shapes=[
                pltpu.VMEM((nd, channels, 2, local_dishes, samples), jnp.bfloat16),
                pltpu.VMEM((2, 2, group, dishes, beams), jnp.bfloat16),
                pltpu.VMEM((beams, LANES), jnp.float32),
                pltpu.VMEM((beams // 2 * group, LANES), jnp.float32),
                pltpu.VMEM((groups, devices, group, columns), jnp.bfloat16),
                pltpu.SemaphoreType.DMA((groups,)),
                pltpu.SemaphoreType.DMA((2,)),
                pltpu.SemaphoreType.DMA((groups, nd)),
                pltpu.SemaphoreType.DMA((groups, nd)),
                pltpu.SemaphoreType.DMA((devices,)),
                pltpu.SemaphoreType.DMA((devices,)),
                pltpu.SemaphoreType.DMA((groups,)),
            ],
            compiler_params=pltpu.CompilerParams(has_side_effects=True, vmem_limit_bytes=62 * 1024 * 1024),
        )(vt, beam_weights, spread(flags), 0.05 * spread(sk_bins), onehot, counts)

    in_specs = (
        P(None, "dish", "chan", None),
        P(None, ("chan", "dish"), None, None),
        P("chan"),
        P("chan"),
        P(),
    )
    return jax.shard_map(
        body, mesh=mesh, in_specs=in_specs, out_specs=P(None, ("dish", "chan")), check_vma=False
    )
```

time: 1830 us -> 460 us (0.25)
  blocking collectives: 567 us -> 0 us
  Pallas kernels: 0 us -> 420 us
  local copies, waits for them, and re-layouts: 370 us -> 34.3 us
  matrix products: 313 us -> 0 us
  loops' own time: 218 us -> 0 us
  waiting for transfers between devices: 180 us -> 0 us
  other arithmetic: 159 us -> 4.33 us
    all_to_all x2 -> x0, blocking collectives: 555 us -> none  [the longest x1 368 us: body(): lax.all_to_all(lax.all_to_all(blocks, 'dish', split_axis=3, concat_axis=1...]
    pallas_call x0 -> x1, Pallas kernels: none -> 420 us  [body(): pl.pallas_call(functools.partial(kernel, nd, nc, group), out_shape=jax.Sh...]
    dot_general x384 -> x0, matrix products: 313 us -> none  [the longest x128 153 us: channel_average(): jnp.dot(lower, onehot, preferred_element_type=jnp.float32)]
    squeeze x256 -> x0, local copies, waits for them, and re-layouts: 231 us -> none  [the longest x128 118 us: channel_average(): real_rows = jnp.concatenate([weights[0], -weights[1]], axis=0)]
    another operation x1 -> x0, loops' own time: 218 us -> none  [body(): averaged = lax.map(one_channel, jnp.arange(chan_here, dtype=jnp.int32))]
    all_to_all x1 -> x0, waiting for transfers between devices: 180 us -> none  [body(): lax.all_to_all(apply_scale(voltages, scaling), 'dish', split_axis=2, conc...]
    neg x128 -> x0, other arithmetic: 119 us -> none  [channel_average(): real_rows = jnp.concatenate([weights[0], -weights[1]], axis=0)]
    dynamic_slice x128 -> x0, local copies, waits for them, and re-layouts: 73.9 us -> none  [body(): averaged = lax.map(one_channel, jnp.arange(chan_here, dtype=jnp.int32))]
  transfers between devices with their start and end apart: 1 -> 0, of which waited for: 1 -> 0; matrix products, arithmetic and copies ran while one was open for 0% -> 0% of each run, Pallas kernels for 0% -> 0%
where the time goes in v1:
time: 460 us; the launch traced here: 459 us
  Pallas kernels  420 us (91%)
  local copies, waits for them, and re-layouts  34.3 us (7%)
    pallas_call x1, Pallas kernels, body(): pl.pallas_call(functools.partial(kernel, nd, nc, group), out_shape=jax.Sh...  420 us
    transpose x1, local copies, waits for them, and re-layouts, body(): jnp.transpose(voltages, (2, 0, 1, 3))  18.5 us
    unnamed x1, local copies, waits for them, and re-layouts  14.2 us

profile of v1, /device:TPU:0, one launch (start us, length us, event | category | flops | bytes accessed | tf_op | source)
XLA Modules:
  0.0 458.5 jit_solution(17326538206765093662)
XLA Ops:
  0.0 1.4 fusion
  1.4 0.8 dynamic-slice_convert_fusion
  2.1 0.8 convert_multiply_fusion
  2.9 0.8 broadcast_in_dim.7.width_ref
  3.7 0.8 broadcast_in_dim.6.flag_ref
  4.5 1.5 compare_convert_fusion.1.onehot_ref
  6.0 18.5 %copy.6 = bf16[512,2,16,512]{3,2,1,0:T(8,128)(2,1)} copy(bf16[512,2,16,512]{3,0,2,1:T(8,128)(2,1)} %bitcast.4) | data formatting | bytes 33554432 | tf_op jit(solution)/shard_map/transpose | solution.py:194
  24.4 419.9 %shard_map.55 = bf16[4096,2048]{1,0:T(8,128)(2,1)} custom-call(bf16[4,128,2,16,512]{4,3,2,1,0:T(8,128)(2,1)} %bitcast.3, bf16[2,128,64,1024]{3,2,1,0:T(8,128)(2,1)} %w_ref.1, f32[128,1,128]{2,1,0:T(1,128)} %broadcast_in_dim.6.flag_ref, f32[128,1,128]{2,1,0:T(1,128)} %broadcast_in_dim.7.width_ref, bf16[512,128]{1,0:T(8,128)(2,1)} %compare_convert_fusion.1.onehot_ref, ...), custom_call_target="tpu_custom_call" | custom-call | tf_op jit(solution)/shard_map/pallas_call | solution.py:205
  444.4 14.2 %copy.8 = bf16[4096,2048]{1,0:T(8,128)(2,1)} copy(bf16[4096,2048]{1,0:T(8,128)(2,1)} %shard_map.55) | data formatting | bytes 33554432
  (1 shorter events, 0.0 us)

commit v2 on v1

--- a/solution.py
+++ b/solution.py
@@ -14,16 +14,17 @@
 
 def kernel(
     nd, nc, group,
-    vt_ref, w_ref, flag_ref, width_ref, onehot_ref, count_ref,
+    v_ref, w_ref, flag_ref, sk_ref, bin_ref,
     out_ref,
-    volts, wbuf, qbuf, rbuf, stage,
+    volts, fbuf, wbuf, qbuf, rbuf, stage, onehot, counts,
     own_sem, w_sem, send1, recv1, send3, recv3, self_sem,
 ):
-    channels = vt_ref.shape[1]
+    channels = w_ref.shape[1]
+    local_dishes = v_ref.shape[1]
     groups = channels // group
     dishes = w_ref.shape[2]
     beams = w_ref.shape[3]
-    samples = vt_ref.shape[4]
+    samples = v_ref.shape[3]
     devices = nd * nc
     pairs = beams // 2
     own_pairs = pairs // devices
@@ -35,8 +36,8 @@
     def volt_copy(g, off):
         peer = lax.rem(me_d + off, nd)
         return pltpu.make_async_remote_copy(
-            src_ref=vt_ref.at[peer, pl.ds(g * group, group)],
-            dst_ref=volts.at[me_d, pl.ds(g * group, group)],
+            src_ref=v_ref.at[:, :, pl.ds(pl.multiple_of(peer * channels + g * group, group), group)],
+            dst_ref=volts.at[g, me_d],
             send_sem=send1.at[g, off],
             recv_sem=recv1.at[g, off],
             device_id=(peer, me_c),
@@ -45,7 +46,7 @@
 
     def volt_arrival(g, off):
         source = lax.rem(me_d + nd - off, nd)
-        here = volts.at[source, pl.ds(g * group, group)]
+        here = volts.at[g, source]
         return pltpu.make_async_remote_copy(
             src_ref=here, dst_ref=here, send_sem=send1.at[g, off], recv_sem=recv1.at[g, off],
             device_id=(source, me_c), device_id_type=MESH,
@@ -53,7 +54,9 @@
 
     def own_copy(g):
         return pltpu.make_async_copy(
-            vt_ref.at[me_d, pl.ds(g * group, group)], volts.at[me_d, pl.ds(g * group, group)], own_sem.at[g]
+            v_ref.at[:, :, pl.ds(pl.multiple_of(me_d * channels + g * group, group), group)],
+            volts.at[g, me_d],
+            own_sem.at[g],
         )
 
     def weight_copy(g):
@@ -68,6 +71,12 @@
 
     lax.fori_loop(0, groups, start_volts, 0)
     weight_copy(0).start()
+
+    bins = lax.rem(lax.broadcasted_iota(jnp.int32, (LANES, samples), 0), TBINS)
+    matches = jnp.where(bin_ref[...] == bins, 1.0, 0.0).astype(jnp.float32)
+    turned = matches.T
+    onehot[...] = turned.astype(jnp.bfloat16)
+    counts[...] = jnp.sum(turned, axis=0, keepdims=True)
 
     def result_copy(g, off):
         target = lax.rem(me + off, devices)
@@ -103,21 +112,30 @@
             volt_arrival(g, off).wait_recv()
         weight_copy(g).wait()
 
+        for part in range(2):
+            for source in range(nd):
+                rows = local_dishes * group
+                wide = volts[g, source, part].astype(jnp.float32).reshape(rows, samples)
+                for t in range(samples // LANES):
+                    fbuf[t, pl.ds((part * nd + source) * rows, rows), :] = wide[:, t * LANES : (t + 1) * LANES]
+
         def one_channel(i, _):
-            c = g * group + i
-            both = volts[:, c]
-            real = both[:, 0].reshape(dishes, samples)
-            imag = both[:, 1].reshape(dishes, samples)
-            real32 = real.astype(jnp.float32)
-            imag32 = imag.astype(jnp.float32)
+            c = me_d * channels + g * group + i
+            spots = range(samples // LANES)
+            real32 = jnp.concatenate([fbuf[t, pl.ds(i, dishes, stride=group), :] for t in spots], axis=1)
+            imag32 = jnp.concatenate(
+                [fbuf[t, pl.ds(dishes * group + i, dishes, stride=group), :] for t in spots], axis=1
+            )
+            real = real32.astype(jnp.bfloat16)
+            imag = imag32.astype(jnp.bfloat16)
             power = real32 * real32 + imag32 * imag32
             one = jnp.sum(jnp.sum(power, axis=0, keepdims=True), axis=1, keepdims=True) / total
             two = jnp.sum(jnp.sum(power * power, axis=0, keepdims=True), axis=1, keepdims=True) / total
             ratio = two / (one * one + 1e-06)
             excess = (total + 1.0) / (total - 1.0) * (ratio - 1.0) - 1.0
-            width = width_ref[c]
-            scaling = flag_ref[c] * width / (width + excess * excess)
-            factor = scaling * scaling / count_ref[...]
+            width = 0.05 * sk_ref[c].astype(jnp.float32)
+            scaling = flag_ref[c].astype(jnp.float32) * width / (width + excess * excess)
+            factor = scaling * scaling / counts[...]
             right = jnp.concatenate(
                 [jnp.concatenate([real, imag], axis=1), jnp.concatenate([-imag, real], axis=1)], axis=0
             )
@@ -131,7 +149,7 @@
                 re = beam[:, :samples]
                 im = beam[:, samples:]
                 detected = (re * re + im * im).astype(jnp.bfloat16)
-                binned = jnp.dot(detected, onehot_ref[...], preferred_element_type=jnp.float32)
+                binned = jnp.dot(detected, onehot[...], preferred_element_type=jnp.float32)
                 qbuf[pl.ds(at, block), :] = binned * factor
             even = qbuf[pl.ds(0, pairs, stride=2), :]
             odd = qbuf[pl.ds(1, pairs, stride=2), :]
@@ -185,34 +203,29 @@
     nd, nc = mesh.shape["dish"], mesh.shape["chan"]
 
     def body(voltages, beam_weights, flags, sk_bins, bin_of_sample):
-        _, local_dishes, block_channels, samples = voltages.shape
+        _, local_dishes, _, samples = voltages.shape
         _, channels, dishes, beams = beam_weights.shape
         devices = nd * nc
-        group = min(16, channels)
+        group = min(8, channels)
         groups = channels // group
         columns = beams // devices * TBINS
-        vt = jnp.transpose(voltages, (2, 0, 1, 3)).reshape(nd, channels, 2, local_dishes, samples)
-        start = lax.axis_index("dish") * channels
-        spread = lambda x: jnp.broadcast_to(
-            lax.dynamic_slice(x, (start,), (channels,)).astype(jnp.float32)[:, None, None], (channels, 1, LANES)
-        )
-        bins = jnp.arange(LANES, dtype=jnp.int32) % TBINS
-        matches = bin_of_sample[:, None] == bins[None, :]
-        onehot = matches.astype(jnp.bfloat16)
-        counts = jnp.sum(matches.astype(jnp.float32), axis=0, keepdims=True)
         anywhere = pl.BlockSpec(memory_space=pl.ANY)
         local = pl.BlockSpec(memory_space=pltpu.VMEM)
+        scalars = pl.BlockSpec(memory_space=pltpu.SMEM)
         return pl.pallas_call(
             functools.partial(kernel, nd, nc, group),
             out_shape=jax.ShapeDtypeStruct((devices * channels, columns), jnp.bfloat16),
-            in_specs=[anywhere, anywhere, local, local, local, local],
+            in_specs=[anywhere, anywhere, scalars, scalars, local],
             out_specs=anywhere,
             scratch_shapes=[
-                pltpu.VMEM((nd, channels, 2, local_dishes, samples), jnp.bfloat16),
+                pltpu.VMEM((groups, nd, 2, local_dishes, group, samples), jnp.bfloat16),
+                pltpu.VMEM((samples // LANES, 2 * dishes * group, LANES), jnp.float32),
                 pltpu.VMEM((2, 2, group, dishes, beams), jnp.bfloat16),
                 pltpu.VMEM((beams, LANES), jnp.float32),
                 pltpu.VMEM((beams // 2 * group, LANES), jnp.float32),
                 pltpu.VMEM((groups, devices, group, columns), jnp.bfloat16),
+                pltpu.VMEM((samples, LANES), jnp.bfloat16),
+                pltpu.VMEM((1, LANES), jnp.float32),
                 pltpu.SemaphoreType.DMA((groups,)),
                 pltpu.SemaphoreType.DMA((2,)),
                 pltpu.SemaphoreType.DMA((groups, nd)),
@@ -222,7 +235,7 @@
                 pltpu.SemaphoreType.DMA((groups,)),
             ],
             compiler_params=pltpu.CompilerParams(has_side_effects=True, vmem_limit_bytes=62 * 1024 * 1024),
-        )(vt, beam_weights, spread(flags), 0.05 * spread(sk_bins), onehot, counts)
+        )(voltages, beam_weights, flags, sk_bins, bin_of_sample.reshape(1, samples))
 
     in_specs = (
         P(None, "dish", "chan", None),

time: 460 us -> 412 us (0.90)
  Pallas kernels: 420 us -> 397 us
  local copies, waits for them, and re-layouts: 34.3 us -> 14.2 us
    pallas_call x1, Pallas kernels: 420 us -> 397 us  [body(): pl.pallas_call(functools.partial(kernel, nd, nc, group), out_shape=jax.Sh...]
    transpose x1 -> x0, local copies, waits for them, and re-layouts: 18.5 us -> none  [body(): jnp.transpose(voltages, (2, 0, 1, 3))]
where the time goes in v2:
time: 412 us
  Pallas kernels  397 us (96%)
  local copies, waits for them, and re-layouts  14.2 us (3%)
    pallas_call x1, Pallas kernels, body(): pl.pallas_call(functools.partial(kernel, nd, nc, group), out_shape=jax.Sh...  397 us
    unnamed x1, local copies, waits for them, and re-layouts  14.2 us

profile of v2, /device:TPU:0, one launch (start us, length us, event | category | flops | bytes accessed | tf_op | source)
XLA Modules:
  0.0 411.6 jit_solution(428030472936300217)
XLA Ops:
  0.0 397.4 %shard_map.55 = bf16[4096,2048]{1,0:T(8,128)(2,1)} custom-call(bf16[2,16,512,512]{3,2,1,0:T(8,128)(2,1)} %v_ref.1, bf16[2,128,64,1024]{3,2,1,0:T(8,128)(2,1)} %w_ref.1, s32[512]{0:T(512)} %flag_ref.1, s32[512]{0:T(512)} %sk_ref.1, s32[1,512]{1,0:T(1,128)} %bitcast.1), custom_call_target="tpu_custom_call" | custom-call | tf_op jit(solution)/shard_map/pallas_call | solution.py:215
  397.4 14.2 %copy.7 = bf16[4096,2048]{1,0:T(8,128)(2,1)} copy(bf16[4096,2048]{1,0:T(8,128)(2,1)} %shard_map.55) | data formatting | bytes 33554432

commit v3 on v2

--- a/solution.py
+++ b/solution.py
@@ -78,8 +78,7 @@
     onehot[...] = turned.astype(jnp.bfloat16)
     counts[...] = jnp.sum(turned, axis=0, keepdims=True)
 
-    def result_copy(g, off):
-        target = lax.rem(me + off, devices)
+    def result_copy(g, off, target):
         return pltpu.make_async_remote_copy(
             src_ref=stage.at[g, target],
             dst_ref=out_ref.at[pl.ds(pl.multiple_of(my_row + g * group, group), group)],
@@ -96,13 +95,11 @@
             self_sem.at[g],
         )
 
-    lane = lax.broadcasted_iota(jnp.int32, (pairs, LANES), 1)
+    lane = lax.broadcasted_iota(jnp.int32, (min(256, beams) // 2, LANES), 1)
     total = float(dishes * samples)
     block = min(256, beams)
 
-    def one_group(g, _):
-        slot = lax.rem(g, 2)
-
+    def prepare(g):
         @pl.when(g + 1 < groups)
         def _():
             weight_copy(g + 1).start()
@@ -118,6 +115,11 @@
                 wide = volts[g, source, part].astype(jnp.float32).reshape(rows, samples)
                 for t in range(samples // LANES):
                     fbuf[t, pl.ds((part * nd + source) * rows, rows), :] = wide[:, t * LANES : (t + 1) * LANES]
+
+    def work(g, first, count):
+        slot = lax.rem(g, 2)
+        parts = beams // block
+        half = block // 2
 
         def one_channel(i, _):
             c = me_d * channels + g * group + i
@@ -139,7 +141,8 @@
             right = jnp.concatenate(
                 [jnp.concatenate([real, imag], axis=1), jnp.concatenate([-imag, real], axis=1)], axis=0
             )
-            for at in range(0, beams, block):
+            for n in range(count):
+                at = pl.multiple_of((first + n) * block, block)
                 left = jnp.concatenate(
                     [wbuf[slot, 0, i, :, pl.ds(at, block)], wbuf[slot, 1, i, :, pl.ds(at, block)]], axis=0
                 )
@@ -150,13 +153,17 @@
                 im = beam[:, samples:]
                 detected = (re * re + im * im).astype(jnp.bfloat16)
                 binned = jnp.dot(detected, onehot[...], preferred_element_type=jnp.float32)
-                qbuf[pl.ds(at, block), :] = binned * factor
-            even = qbuf[pl.ds(0, pairs, stride=2), :]
-            odd = qbuf[pl.ds(1, pairs, stride=2), :]
-            rbuf[pl.ds(i, pairs, stride=group), :] = jnp.where(lane < TBINS, even, odd)
+                qbuf[pl.ds(n * block, block), :] = binned * factor
+                even = qbuf[pl.ds(n * block, half, stride=2), :]
+                odd = qbuf[pl.ds(n * block + 1, half, stride=2), :]
+                rbuf[pl.ds((first + n) * half * group + i, half, stride=group), :] = jnp.where(
+                    lane < TBINS, even, odd
+                )
             return 0
 
         lax.fori_loop(0, group, one_channel, 0)
+        low = first * (devices // parts)
+        served = count * (devices // parts)
 
         def one_target(j, _):
             for p in range(own_pairs):
@@ -164,17 +171,39 @@
                 stage[g, j, :, pl.ds(p * LANES, LANES)] = rbuf[pl.ds(row, group), :].astype(jnp.bfloat16)
             return 0
 
-        lax.fori_loop(0, devices, one_target, 0)
-
-        def send(off, _):
-            result_copy(g, off).start()
+        lax.fori_loop(low, low + served, one_target, 0)
+
+        def send(k, _):
+            target = low + lax.rem(me + 1 + k, served)
+            off = lax.rem(target - me + devices, devices)
+
+            @pl.when(off != 0)
+            def _():
+                result_copy(g, off, target).start()
+
+            @pl.when(off == 0)
+            def _():
+                self_copy(g).start()
+
             return 0
 
-        lax.fori_loop(1, devices, send, 0)
-        self_copy(g).start()
-        return 0
-
-    lax.fori_loop(0, groups, one_group, 0)
+        lax.fori_loop(0, served, send, 0)
+
+    parts = beams // block
+    prepare(0)
+
+    def one_part(b, _):
+        work(0, lax.rem(me_d + b, parts), 1)
+        return 0
+
+    lax.fori_loop(0, parts, one_part, 0)
+
+    def one_group(g, _):
+        prepare(g)
+        work(g, 0, parts)
+        return 0
+
+    lax.fori_loop(1, groups, one_group, 0)
 
     def finish(g, _):
         for off in range(1, nd):
@@ -214,9 +243,9 @@
         scalars = pl.BlockSpec(memory_space=pltpu.SMEM)
         return pl.pallas_call(
             functools.partial(kernel, nd, nc, group),
-            out_shape=jax.ShapeDtypeStruct((devices * channels, columns), jnp.bfloat16),
+            out_shape=pltpu.VMEM((devices * channels, columns), jnp.bfloat16),
             in_specs=[anywhere, anywhere, scalars, scalars, local],
-            out_specs=anywhere,
+            out_specs=local,
             scratch_shapes=[
                 pltpu.VMEM((groups, nd, 2, local_dishes, group, samples), jnp.bfloat16),
                 pltpu.VMEM((samples // LANES, 2 * dishes * group, LANES), jnp.float32),
@@ -234,7 +263,7 @@
                 pltpu.SemaphoreType.DMA((devices,)),
                 pltpu.SemaphoreType.DMA((groups,)),
             ],
-            compiler_params=pltpu.CompilerParams(has_side_effects=True, vmem_limit_bytes=62 * 1024 * 1024),
+            compiler_params=pltpu.CompilerParams(has_side_effects=True, vmem_limit_bytes=46 * 1024 * 1024),
         )(voltages, beam_weights, flags, sk_bins, bin_of_sample.reshape(1, samples))
 
     in_specs = (

time: 412 us -> 399 us (0.968)
  local copies, waits for them, and re-layouts: 14.2 us -> 6.16 us
    unnamed x1, local copies, waits for them, and re-layouts: 14.2 us -> 6.16 us
    pallas_call x1, Pallas kernels: 397 us -> 393 us  [body(): pl.pallas_call(functools.partial(kernel, nd, nc, group), out_shape=pltpu....]
where the time goes in v3:
time: 399 us
  Pallas kernels  393 us (98%)
  local copies, waits for them, and re-layouts  6.16 us (2%)
    pallas_call x1, Pallas kernels, body(): pl.pallas_call(functools.partial(kernel, nd, nc, group), out_shape=pltpu....  393 us

profile of v3, /device:TPU:0, one launch (start us, length us, event | category | flops | bytes accessed | tf_op | source)
XLA Modules:
  0.0 398.7 jit_solution(15736733335337686518)
XLA Ops:
  0.0 392.5 %shard_map.55 = bf16[4096,2048]{1,0:T(8,128)(2,1)S(1)} custom-call(bf16[2,16,512,512]{3,2,1,0:T(8,128)(2,1)} %v_ref.1, bf16[2,128,64,1024]{3,2,1,0:T(8,128)(2,1)} %w_ref.1, s32[512]{0:T(512)} %flag_ref.1, s32[512]{0:T(512)} %sk_ref.1, s32[1,512]{1,0:T(1,128)} %bitcast.1), custom_call_target="tpu_custom_call" | custom-call | tf_op jit(solution)/shard_map/pallas_call | solution.py:244
  392.5 6.2 %copy.7 = bf16[4096,2048]{1,0:T(8,128)(2,1)} copy(bf16[4096,2048]{1,0:T(8,128)(2,1)S(1)} %shard_map.55) | data formatting | bytes 33554432
